TPU v7x, 32 devices: a whole 2x2x4 slice. The times are simulated.
32 devices in a mesh: dp: 8 (over z, x), expert: 4 (over y, core).
Axes of the slice: x: 2, y: 2, z: 4, core: 2. Of those that a mesh axis runs over, the one named last changes fastest.
Arguments:
- inputs: bfloat16 [32, 128, 2048], P(('dp', 'expert')), may hold values from -6 to 6
- cotangent: bfloat16 [32, 128, 2048], P(('dp', 'expert')), may hold values from -6 to 6
- lengths: int32 [32], P('dp'), may hold values from 1 to 128, 3072 in all
- dealing: int32 [8, 4], P('dp'), may hold values from 0 to 3, each once within a row
- routes: int32 [32, 128, 8], P(('dp', 'expert')), may hold values from 0 to 15, all different within a row; in each aligned block of 128 rows (0 to 127, 128 to 255, ..., all dimensions but the last counted through in order) at most 72 rows name the same one
- gate_values: float32 [32, 128, 8], P(('dp', 'expert')), may hold values from 0.25 to 0.75
- attn_gain: float32 [2048], replicated, may hold values from 0.1 to 1.9
- w_query: float32 [2048, 2048], P(('dp', 'expert')), may hold values from -0.125 to 0.125
- w_key: float32 [2048, 2048], P(('dp', 'expert')), may hold values from -0.125 to 0.125
- w_value: float32 [2048, 2048], P(('dp', 'expert')), may hold values from -0.125 to 0.125
- query_gain: float32 [2048], replicated, may hold values from 0.1 to 1.9
- key_gain: float32 [2048], replicated, may hold values from 0.1 to 1.9
- w_out: float32 [2048, 2048], P(('dp', 'expert')), may hold values from -0.5 to 0.5
- ffn_gain: float32 [2048], replicated, may hold values from 0.1 to 1.9
- w_gate: float32 [16, 2048, 1024], P('expert', 'dp'), may hold values from -0.125 to 0.125
- w_up: float32 [16, 2048, 1024], P('expert', 'dp'), may hold values from -0.125 to 0.125
- w_down: float32 [16, 1024, 2048], P('expert', 'dp'), may hold values from -0.1875 to 0.1875
Outputs:
- layer_out: bfloat16 [32, 128, 2048], P(('dp', 'expert'))
- grad_inputs: bfloat16 [32, 128, 2048], P(('dp', 'expert'))
- grad_attn_gain: float32 [2048], P(('dp', 'expert'))
- grad_w_query: float32 [2048, 2048], P(('dp', 'expert'))
- grad_w_key: float32 [2048, 2048], P(('dp', 'expert'))
- grad_w_value: float32 [2048, 2048], P(('dp', 'expert'))
- grad_query_gain: float32 [2048], P(('dp', 'expert'))
- grad_key_gain: float32 [2048], P(('dp', 'expert'))
- grad_w_out: float32 [2048, 2048], P(('dp', 'expert'))
- grad_ffn_gain: float32 [2048], P(('dp', 'expert'))
- grad_w_gate: float32 [16, 2048, 1024], P('expert', 'dp')
- grad_w_up: float32 [16, 2048, 1024], P('expert', 'dp')
- grad_w_down: float32 [16, 1024, 2048], P('expert', 'dp')
Inputs may be any that keep to these rules, and one draw needn't show every extreme that they name: `lengths`: the longest sequence has exactly 128 tokens. `dealing`: each row names every sequence of its group once. `routes`: each token names 8 different experts; within one dealt sequence no expert is named more than 72 times, and some sequence reaches 72 in every draw.
All inputs are finite; a program needn't handle non-finite values. No bound on the sum of `lengths` on one device may be relied on, other than what follows from the above.
Results may differ from a plain program's by a relative error of at most 0.015.
Values may be sent and summed in bfloat16 or wider, within the bound.
A program may use at most 384 MiB of HBM per device.

v0:
```python
import math
import jax
import jax.numpy as jnp
from jax import lax
from jax.sharding import PartitionSpec as P

HEADS = 16
epsilon = 1e-05


def norm_scale(values):
    return lax.rsqrt(jnp.mean(values * values, axis=-1, keepdims=True) + epsilon)


def norm_back(normed, row_scale, incoming):
    return row_scale * (incoming - normed * jnp.mean(incoming * normed, axis=-1, keepdims=True))


def angle_tables(length_rows, head_size):
    half_size = head_size // 2
    position = jnp.arange(length_rows, dtype=jnp.float32)[:, None]
    inverse = jnp.exp(
        jnp.arange(half_size, dtype=jnp.float32) * (-2.0 * math.log(10000.0) / head_size)
    )
    angles = position * inverse[None, :]
    return (jnp.cos(angles)[:, None, :], jnp.sin(angles)[:, None, :])


def rotate_pairs(values, cosine, sine_table):
    half_size = values.shape[-1] // 2
    first = values[..., :half_size]
    second = values[..., half_size:]
    return jnp.concatenate(
        [first * cosine - second * sine_table, second * cosine + first * sine_table], axis=-1
    )


def route_tables(expert_picks, experts, capacity):
    flat_picks = expert_picks.reshape(-1)
    onehot = (flat_picks[:, None] == jnp.arange(experts, dtype=jnp.int32)[None, :]).astype(
        jnp.int32
    )
    before = jnp.cumsum(onehot, axis=0) - onehot
    rank_within = jnp.sum(before * onehot, axis=1)
    slot_place = flat_picks * capacity + rank_within
    pair_count = flat_picks.shape[0]
    owner_pair = (
        jnp.zeros((experts * capacity,), jnp.int32)
        .at[slot_place]
        .set(jnp.arange(pair_count, dtype=jnp.int32))
    )
    filled = jnp.zeros((experts * capacity,), jnp.int32).at[slot_place].set(1)
    return (slot_place, owner_pair, filled)


def expert_front(received, gate_mat, up_mat):
    gate_pre = jnp.einsum("emd,edf->emf", received, gate_mat, preferred_element_type=jnp.float32)
    up_pre = jnp.einsum("emd,edf->emf", received, up_mat, preferred_element_type=jnp.float32)
    hidden_act = (jax.nn.silu(gate_pre) * up_pre).astype(jnp.bfloat16)
    return (gate_pre, up_pre, hidden_act)


def per_device(
    inputs,
    cotangent,
    lengths,
    dealing,
    routes,
    gate_values,
    attn_gain,
    w_query,
    w_key,
    w_value,
    query_gain,
    key_gain,
    w_out,
    ffn_gain,
    w_gate,
    w_up,
    w_down,
):
    group_size = lax.axis_size("expert")
    position = lax.axis_index("expert")
    deal_order = dealing[0]
    source = deal_order[position]
    dealt_rows = (
        lax.all_gather(inputs, "expert", axis=0, tiled=True),
        lax.all_gather(cotangent, "expert", axis=0, tiled=True),
    )
    seq_inputs = lax.dynamic_index_in_dim(dealt_rows[0], source, 0, keepdims=False).astype(
        jnp.float32
    )
    seq_grads = lax.dynamic_index_in_dim(dealt_rows[1], source, 0, keepdims=False).astype(
        jnp.float32
    )
    seq_length = lengths[source]
    length_rows, width = seq_inputs.shape
    head_size = width // HEADS
    attn_mats = (
        lax.all_gather(w_query.astype(jnp.bfloat16), ("dp", "expert"), axis=0, tiled=True),
        lax.all_gather(w_key.astype(jnp.bfloat16), ("dp", "expert"), axis=0, tiled=True),
        lax.all_gather(w_value.astype(jnp.bfloat16), ("dp", "expert"), axis=0, tiled=True),
        lax.all_gather(w_out.astype(jnp.bfloat16), ("dp", "expert"), axis=0, tiled=True),
    )
    query_mat, key_mat, value_mat, out_mat = attn_mats
    scale_in = norm_scale(seq_inputs)
    normed_in = seq_inputs * scale_in
    hidden_in = (normed_in * attn_gain).astype(jnp.bfloat16)
    query_raw = jnp.dot(hidden_in, query_mat, preferred_element_type=jnp.float32)
    key_raw = jnp.dot(hidden_in, key_mat, preferred_element_type=jnp.float32)
    values = jnp.dot(hidden_in, value_mat, preferred_element_type=jnp.float32).astype(jnp.bfloat16)
    cosine, sine_table = angle_tables(length_rows, head_size)
    query_scale = norm_scale(query_raw)
    query_normed = query_raw * query_scale
    key_scale = norm_scale(key_raw)
    key_normed = key_raw * key_scale
    queries = rotate_pairs(
        (query_normed * query_gain).reshape(length_rows, HEADS, head_size), cosine, sine_table
    ).astype(jnp.bfloat16)
    key_rows = rotate_pairs(
        (key_normed * key_gain).reshape(length_rows, HEADS, head_size), cosine, sine_table
    ).astype(jnp.bfloat16)
    head_values = values.reshape(length_rows, HEADS, head_size)
    factor = head_size ** (-0.5)
    row_index = jnp.arange(length_rows, dtype=jnp.int32)[:, None]
    col_index = jnp.arange(length_rows, dtype=jnp.int32)[None, :]
    visible = (col_index <= row_index) & (col_index < seq_length)
    scores = (
        jnp.einsum("ihd,jhd->hij", queries, key_rows, preferred_element_type=jnp.float32) * factor
    )
    scores = jnp.where(visible[None], scores, -1e30)
    weights = jax.nn.softmax(scores, axis=-1)
    weights_low = weights.astype(jnp.bfloat16)
    attended = jnp.einsum(
        "hij,jhd->ihd", weights_low, head_values, preferred_element_type=jnp.float32
    )
    attended = attended.reshape(length_rows, width).astype(jnp.bfloat16)
    residual = seq_inputs + jnp.dot(attended, out_mat, preferred_element_type=jnp.float32)
    scale_mid = norm_scale(residual)
    normed_mid = residual * scale_mid
    hidden_mid = (normed_mid * ffn_gain).astype(jnp.bfloat16)
    local_experts = w_gate.shape[0]
    experts = local_experts * group_size
    top_count = routes.shape[2]
    capacity = length_rows * top_count * 9 // (8 * experts)
    slot_place, owner_pair, filled = route_tables(routes[0], experts, capacity)
    live_slot = filled[:, None] > 0
    token_of_slot = owner_pair // top_count
    sending = jnp.where(live_slot, hidden_mid[token_of_slot], jnp.zeros((), jnp.bfloat16))
    sending = sending.reshape(group_size, local_experts, capacity, width)
    received = lax.all_to_all(sending, "expert", split_axis=0, concat_axis=2, tiled=True)[0]
    expert_mats = (
        lax.all_gather(w_gate.astype(jnp.bfloat16), "dp", axis=1, tiled=True),
        lax.all_gather(w_up.astype(jnp.bfloat16), "dp", axis=1, tiled=True),
        lax.all_gather(w_down.astype(jnp.bfloat16), "dp", axis=1, tiled=True),
    )
    gate_mat, up_mat, down_mat = expert_mats
    gate_pre, up_pre, hidden_act = expert_front(received, gate_mat, up_mat)
    expert_out = jnp.einsum(
        "emf,efd->emd", hidden_act, down_mat, preferred_element_type=jnp.float32
    ).astype(jnp.bfloat16)
    returned = lax.all_to_all(
        expert_out[None], "expert", split_axis=2, concat_axis=0, tiled=True
    ).reshape(experts * capacity, width)
    picked = returned[slot_place].reshape(length_rows, top_count, width)
    mixture = jnp.sum(gate_values[0][:, :, None] * picked.astype(jnp.float32), axis=1)
    layer_rows = (residual + mixture).astype(jnp.bfloat16)
    flat_gates = gate_values[0].reshape(-1)
    slot_grads = jnp.where(
        live_slot, flat_gates[owner_pair][:, None] * seq_grads[token_of_slot], 0.0
    ).astype(jnp.bfloat16)
    slot_grads = slot_grads.reshape(group_size, local_experts, capacity, width)
    out_grads = lax.all_to_all(slot_grads, "expert", split_axis=0, concat_axis=2, tiled=True)[0]
    gate_mat, up_mat, down_mat = (
        lax.all_gather(w_gate.astype(jnp.bfloat16), "dp", axis=1, tiled=True),
        lax.all_gather(w_up.astype(jnp.bfloat16), "dp", axis=1, tiled=True),
        lax.all_gather(w_down.astype(jnp.bfloat16), "dp", axis=1, tiled=True),
    )
    grad_hidden = jnp.einsum(
        "emd,efd->emf", out_grads, down_mat, preferred_element_type=jnp.float32
    )
    sigmoid_gate = jax.nn.sigmoid(gate_pre)
    grad_gate_pre = (
        grad_hidden * up_pre * sigmoid_gate * (1.0 + gate_pre * (1.0 - sigmoid_gate))
    ).astype(jnp.bfloat16)
    grad_up_pre = (grad_hidden * gate_pre * sigmoid_gate).astype(jnp.bfloat16)
    grad_slots = jnp.einsum(
        "emf,edf->emd", grad_gate_pre, gate_mat, preferred_element_type=jnp.float32
    )
    grad_slots = (
        grad_slots
        + jnp.einsum("emf,edf->emd", grad_up_pre, up_mat, preferred_element_type=jnp.float32)
    ).astype(jnp.bfloat16)
    grad_down = jnp.einsum(
        "emf,emd->efd", hidden_act, out_grads, preferred_element_type=jnp.float32
    )
    grad_gate = jnp.einsum(
        "emd,emf->edf", received, grad_gate_pre, preferred_element_type=jnp.float32
    )
    grad_up = jnp.einsum("emd,emf->edf", received, grad_up_pre, preferred_element_type=jnp.float32)
    expert_summed = (
        lax.psum_scatter(
            grad_gate.astype(jnp.bfloat16), "dp", scatter_dimension=1, tiled=True
        ).astype(jnp.float32),
        lax.psum_scatter(
            grad_up.astype(jnp.bfloat16), "dp", scatter_dimension=1, tiled=True
        ).astype(jnp.float32),
        lax.psum_scatter(
            grad_down.astype(jnp.bfloat16), "dp", scatter_dimension=1, tiled=True
        ).astype(jnp.float32),
    )
    sent_back = lax.all_to_all(
        grad_slots[None], "expert", split_axis=2, concat_axis=0, tiled=True
    ).reshape(experts * capacity, width)
    grad_mid = jnp.sum(
        sent_back[slot_place].reshape(length_rows, top_count, width).astype(jnp.float32), axis=1
    )
    ffn_gain_part = jnp.sum(grad_mid * normed_mid, axis=0)
    grad_resid = seq_grads + norm_back(normed_mid, scale_mid, grad_mid * ffn_gain)
    resid_low = grad_resid.astype(jnp.bfloat16)
    grad_out_mat = jnp.einsum("td,te->de", attended, resid_low, preferred_element_type=jnp.float32)
    grad_attended = jnp.einsum(
        "te,de->td", resid_low, out_mat, preferred_element_type=jnp.float32
    ).astype(jnp.bfloat16)
    grad_attended = grad_attended.reshape(length_rows, HEADS, head_size)
    grad_values = jnp.einsum(
        "hij,ihd->jhd", weights_low, grad_attended, preferred_element_type=jnp.float32
    )
    grad_values = grad_values.reshape(length_rows, width).astype(jnp.bfloat16)
    grad_weights = jnp.einsum(
        "ihd,jhd->hij", grad_attended, head_values, preferred_element_type=jnp.float32
    )
    grad_scores = (
        weights * (grad_weights - jnp.sum(weights * grad_weights, axis=-1, keepdims=True))
    ).astype(jnp.bfloat16)
    grad_queries = (
        jnp.einsum("hij,jhd->ihd", grad_scores, key_rows, preferred_element_type=jnp.float32)
        * factor
    )
    grad_keys = (
        jnp.einsum("hij,ihd->jhd", grad_scores, queries, preferred_element_type=jnp.float32)
        * factor
    )
    query_turned = rotate_pairs(grad_queries, cosine, -sine_table).reshape(length_rows, width)
    key_turned = rotate_pairs(grad_keys, cosine, -sine_table).reshape(length_rows, width)
    query_gain_part = jnp.sum(query_turned * query_normed, axis=0)
    key_gain_part = jnp.sum(key_turned * key_normed, axis=0)
    grad_query_raw = norm_back(query_normed, query_scale, query_turned * query_gain).astype(
        jnp.bfloat16
    )
    grad_key_raw = norm_back(key_normed, key_scale, key_turned * key_gain).astype(jnp.bfloat16)
    grad_query_mat = jnp.einsum(
        "td,te->de", hidden_in, grad_query_raw, preferred_element_type=jnp.float32
    )
    grad_key_mat = jnp.einsum(
        "td,te->de", hidden_in, grad_key_raw, preferred_element_type=jnp.float32
    )
    grad_value_mat = jnp.einsum(
        "td,te->de", hidden_in, grad_values, preferred_element_type=jnp.float32
    )
    grad_hidden_in = jnp.einsum(
        "te,de->td", grad_query_raw, query_mat, preferred_element_type=jnp.float32
    )
    grad_hidden_in = grad_hidden_in + jnp.einsum(
        "te,de->td", grad_key_raw, key_mat, preferred_element_type=jnp.float32
    )
    grad_hidden_in = grad_hidden_in + jnp.einsum(
        "te,de->td", grad_values, value_mat, preferred_element_type=jnp.float32
    )
    attn_gain_part = jnp.sum(grad_hidden_in * normed_in, axis=0)
    grad_seq = grad_resid + norm_back(normed_in, scale_in, grad_hidden_in * attn_gain)
    attn_summed = (
        lax.psum_scatter(grad_query_mat, ("dp", "expert"), scatter_dimension=0, tiled=True),
        lax.psum_scatter(grad_key_mat, ("dp", "expert"), scatter_dimension=0, tiled=True),
        lax.psum_scatter(grad_value_mat, ("dp", "expert"), scatter_dimension=0, tiled=True),
        lax.psum_scatter(grad_out_mat, ("dp", "expert"), scatter_dimension=0, tiled=True),
        lax.psum_scatter(attn_gain_part, ("dp", "expert"), scatter_dimension=0, tiled=True),
        lax.psum_scatter(query_gain_part, ("dp", "expert"), scatter_dimension=0, tiled=True),
        lax.psum_scatter(key_gain_part, ("dp", "expert"), scatter_dimension=0, tiled=True),
        lax.psum_scatter(ffn_gain_part, ("dp", "expert"), scatter_dimension=0, tiled=True),
    )
    back_rows = (
        lax.all_gather(layer_rows[None], "expert", axis=0, tiled=True),
        lax.all_gather(grad_seq.astype(jnp.bfloat16)[None], "expert", axis=0, tiled=True),
    )
    holder = jnp.sum(jnp.where(deal_order == position, jnp.arange(group_size, dtype=jnp.int32), 0))
    out_rows = lax.dynamic_slice_in_dim(back_rows[0], holder, 1, 0)
    grad_rows_out = lax.dynamic_slice_in_dim(back_rows[1], holder, 1, 0)
    return (
        out_rows,
        grad_rows_out,
        attn_summed[4],
        attn_summed[0],
        attn_summed[1],
        attn_summed[2],
        attn_summed[5],
        attn_summed[6],
        attn_summed[3],
        attn_summed[7],
        expert_summed[0],
        expert_summed[1],
        expert_summed[2],
    )


def solution(mesh):
    return jax.shard_map(
        per_device,
        mesh=mesh,
        in_specs=(
            P(("dp", "expert"), None, None),
            P(("dp", "expert"), None, None),
            P("dp"),
            P("dp", None),
            P(("dp", "expert"), None, None),
            P(("dp", "expert"), None, None),
            P(),
            P(("dp", "expert"), None),
            P(("dp", "expert"), None),
            P(("dp", "expert"), None),
            P(),
            P(),
            P(("dp", "expert"), None),
            P(),
            P("expert", "dp", None),
            P("expert", "dp", None),
            P("expert", "dp", None),
        ),
        out_specs=(
            P(("dp", "expert"), None, None),
            P(("dp", "expert"), None, None),
            P(("dp", "expert")),
            P(("dp", "expert"), None),
            P(("dp", "expert"), None),
            P(("dp", "expert"), None),
            P(("dp", "expert")),
            P(("dp", "expert")),
            P(("dp", "expert"), None),
            P(("dp", "expert")),
            P("expert", "dp", None),
            P("expert", "dp", None),
            P("expert", "dp", None),
        ),
        check_vma=False,
    )
```

profile of v0, /device:TPU:3, one launch (start us, length us, event | category | flops | bytes accessed | tf_op | source)
XLA Modules:
  0.0 2965.7 jit_solution(5224413650591121145)
XLA Ops:
  53.2 6.7 gather_fusion.3
  60.0 6.8 select_convert_fusion
  66.8 6.3 all-to-all-start.2
  74.4 81.8 %all-gather.20.cloned.1.call-done = bf16[2048,2048]{1,0:T(8,128)(2,1)} async-done(((bf16[64,2048]{1,0:T(8,128)(2,1)}), bf16[2048,2048]{1,0:T(8,128)(2,1)}) %all-gather.20.cloned.1.call-update) | async-done | bytes 8388624 | tf_op jit(solution)/shard_map/all_gather | solution.py:101
  162.5 73.0 %all-gather.18.cloned.1.call-done = bf16[2048,2048]{1,0:T(8,128)(2,1)} async-done(((bf16[64,2048]{1,0:T(8,128)(2,1)}), bf16[2048,2048]{1,0:T(8,128)(2,1)}) %all-gather.18.cloned.1.call-update) | async-done | bytes 8388624 | tf_op jit(solution)/shard_map/all_gather | solution.py:100
  248.1 66.8 %all-gather.16.cloned.1.call-done = bf16[2048,2048]{1,0:T(8,128)(2,1)} async-done(((bf16[64,2048]{1,0:T(8,128)(2,1)}), bf16[2048,2048]{1,0:T(8,128)(2,1)}) %all-gather.16.cloned.1.call-update) | async-done | bytes 8388624 | tf_op jit(solution)/shard_map/all_gather | solution.py:102
  314.9 5.5 fusion.14
  322.9 71.5 %all-gather.22.cloned.1.call-done = bf16[2048,2048]{1,0:T(8,128)(2,1)} async-done(((bf16[64,2048]{1,0:T(8,128)(2,1)}), bf16[2048,2048]{1,0:T(8,128)(2,1)}) %all-gather.22.cloned.1.call-update) | async-done | bytes 8388624 | tf_op jit(solution)/shard_map/all_gather | solution.py:103
  399.4 6.0 gather_fusion
  405.4 5.4 broadcast_select_fusion
  416.1 5.4 copy.102
  421.5 47.6 %all-to-all-done = bf16[4,4,72,2048]{3,2,1,0:T(8,128)(2,1)} async-done(((bf16[4,4,72,2048]{3,2,1,0:T(8,128)(2,1)}), bf16[4,4,72,2048]{3,2,1,0:T(8,128)(2,1)}, u32[]{:S(2)}, u32[]{:S(2)}) %all-to-all-start) | async-done | bytes 4718624 | tf_op jit(solution)/shard_map/all_to_all | solution.py:151
  474.4 147.3 %all-gather.24.cloned.1.call-done = bf16[4,2048,1024]{2,1,0:T(8,128)(2,1)} async-done(((bf16[4,256,1024]{2,1,0:T(8,128)(2,1)}), bf16[4,2048,1024]{2,1,0:T(8,128)(2,1)}) %all-gather.24.cloned.1.call-update) | async-done | bytes 16777232 | tf_op jit(solution)/shard_map/all_gather | solution.py:153
  621.7 13.3 fusion.79
  634.9 215.3 %all-gather.26.cloned.1.call-done = bf16[4,2048,1024]{2,1,0:T(8,128)(2,1)} async-done(((bf16[4,256,1024]{2,1,0:T(8,128)(2,1)}), bf16[4,2048,1024]{2,1,0:T(8,128)(2,1)}) %all-gather.26.cloned.1.call-update) | async-done | bytes 16777232 | tf_op jit(solution)/shard_map/all_gather | solution.py:154
  850.2 13.2 fusion.80
  863.4 215.4 %all-gather.28.cloned.1.call-done = bf16[4,1024,2048]{2,1,0:T(8,128)(2,1)} async-done(((bf16[4,128,2048]{2,1,0:T(8,128)(2,1)}), bf16[4,1024,2048]{2,1,0:T(8,128)(2,1)}) %all-gather.28.cloned.1.call-update) | async-done | bytes 16777232 | tf_op jit(solution)/shard_map/all_gather | solution.py:155
  1078.8 15.1 multiply_convert_fusion
  1093.9 11.5 fusion.81
  1105.4 13.6 fusion.2
  1119.0 8.1 copy.103
  1127.2 6.4 all-to-all-start.3
  1133.6 11.5 convert_bitcast_fusion
  1145.0 5.8 copy.99
  1150.8 35.7 %all-to-all-done.3 = bf16[1,4,288,2048]{3,1,0,2:T(4,128)(2,1)} async-done(((bf16[1,4,288,2048]{3,1,0,2:T(4,128)(2,1)}), bf16[1,4,288,2048]{3,1,0,2:T(4,128)(2,1)}, u32[]{:S(2)}, u32[]{:S(2)}) %all-to-all-start.3) | async-done | bytes 4718624 | tf_op jit(solution)/shard_map/all_to_all | solution.py:212
  1186.6 5.8 all-to-all-start.1
  1192.5 7.2 copy.104
  1199.6 11.9 gather_fusion.4
  1216.9 28.4 all-to-all-done.1
  1245.4 7.1 copy.100
  1252.5 11.9 gather_fusion.1
  1264.4 6.5 fusion.1
  1273.2 7.2 convolution_convert_fusion.3
  1304.9 14.7 convolution_convert_fusion.2
  1319.7 14.9 convolution_convert_fusion.1
  1334.7 15.5 convolution_convert_fusion
  1350.3 9.1 fusion.37
  1360.4 8.2 fusion.28
  1369.7 8.3 fusion.67
  1379.0 8.3 fusion.69
  1390.5 42.1 %all-reduce.4 = (f32[2048]{0:T(1024)S(1)}, f32[2048]{0:T(1024)S(1)}, f32[2048]{0:T(1024)S(1)}, f32[2048]{0:T(1024)S(1)}) all-reduce(f32[2048]{0:T(1024)S(1)} %get-tuple-element.13, f32[2048]{0:T(1024)S(1)} %get-tuple-element.19, f32[2048]{0:T(1024)S(1)} %get-tuple-element.17, ...), channel_id=4, replica_groups=mesh['dp'=8,'expert'=4] {'dp','expert'}, use_global_device_ids=true, to_apply=%region_20.21.clone | all-reduce | flops 8192 | bytes 65536
  1438.8 198.7 %reduce-scatter.16.cloned.1.call-done = bf16[4,256,1024]{2,1,0:T(8,128)(2,1)} async-done(((bf16[4,2048,1024]{2,1,0:T(8,128)(2,1)}), bf16[4,256,1024]{2,1,0:T(8,128)(2,1)}) %reduce-scatter.16.cloned.1.call-update) | async-done | bytes 2097168 | tf_op jit(solution)/shard_map/reduce_scatter | solution.py:202
  1641.5 281.9 %reduce-scatter.18.cloned.1.call-done = bf16[4,256,1024]{2,1,0:T(8,128)(2,1)} async-done(((bf16[4,2048,1024]{2,1,0:T(8,128)(2,1)}), bf16[4,256,1024]{2,1,0:T(8,128)(2,1)}) %reduce-scatter.18.cloned.1.call-update) | async-done | bytes 2097168 | tf_op jit(solution)/shard_map/reduce_scatter | solution.py:205
  1927.5 281.3 %reduce-scatter.20.cloned.1.call-done = bf16[4,128,2048]{2,1,0:T(8,128)(2,1)} async-done(((bf16[4,1024,2048]{2,1,0:T(8,128)(2,1)}), bf16[4,128,2048]{2,1,0:T(8,128)(2,1)}) %reduce-scatter.20.cloned.1.call-update) | async-done | bytes 2097168 | tf_op jit(solution)/shard_map/reduce_scatter | solution.py:208
  2213.0 183.3 %reduce-scatter.14.cloned.1.call-done = f32[64,2048]{1,0:T(8,128)} async-done(((f32[2048,2048]{1,0:T(8,128)}), f32[64,2048]{1,0:T(8,128)}) %reduce-scatter.14.cloned.1.call-update) | async-done | bytes 524304 | tf_op jit(solution)/shard_map/reduce_scatter | solution.py:276
  2396.3 187.4 %reduce-scatter.12.cloned.1.call-done = f32[64,2048]{1,0:T(8,128)} async-done(((f32[2048,2048]{1,0:T(8,128)}), f32[64,2048]{1,0:T(8,128)}) %reduce-scatter.12.cloned.1.call-update) | async-done | bytes 524304 | tf_op jit(solution)/shard_map/reduce_scatter | solution.py:275
  2583.8 186.7 %reduce-scatter.10.cloned.1.call-done = f32[64,2048]{1,0:T(8,128)} async-done(((f32[2048,2048]{1,0:T(8,128)}), f32[64,2048]{1,0:T(8,128)}) %reduce-scatter.10.cloned.1.call-update) | async-done | bytes 524304 | tf_op jit(solution)/shard_map/reduce_scatter | solution.py:274
  2770.5 188.1 %reduce-scatter.8.cloned.1.call-done = f32[64,2048]{1,0:T(8,128)} async-done(((f32[2048,2048]{1,0:T(8,128)}), f32[64,2048]{1,0:T(8,128)}) %reduce-scatter.8.cloned.1.call-update) | async-done | bytes 524304 | tf_op jit(solution)/shard_map/reduce_scatter | solution.py:273
  (246 shorter events, 136.6 us)
Async XLA Ops:
  7.2 44.9 %all-gather.30.cloned.1.call-start = ((), (), s32[]{:S(2)}) async-start(), calls=%async_computation.19 | async-start | bytes 2621440 | tf_op jit(solution)/shard_map/all_gather | solution.py:88
  7.9 65.2 %all-gather.14.cloned.1.call-start = ((), (), s32[]{:S(2)}) async-start(), calls=%async_computation.11 | async-start | bytes 2621440 | tf_op jit(solution)/shard_map/all_gather | solution.py:87
  8.7 147.5 %all-gather.20.cloned.1.call-start = ((), (), s32[]{:S(2)}) async-start(), calls=%async_computation.14 | async-start | bytes 8650752 | tf_op jit(solution)/shard_map/all_gather | solution.py:101
  10.5 225.0 %all-gather.18.cloned.1.call-start = ((), (), s32[]{:S(2)}) async-start(), calls=%async_computation.13 | async-start | bytes 8650752 | tf_op jit(solution)/shard_map/all_gather | solution.py:100
  12.4 302.6 %all-gather.16.cloned.1.call-start = ((), (), s32[]{:S(2)}) async-start(), calls=%async_computation.12 | async-start | bytes 8650752 | tf_op jit(solution)/shard_map/all_gather | solution.py:102
  14.2 380.2 %all-gather.22.cloned.1.call-start = ((), (), s32[]{:S(2)}) async-start(), calls=%async_computation.15 | async-start | bytes 8650752 | tf_op jit(solution)/shard_map/all_gather | solution.py:103
  16.1 605.6 %all-gather.24.cloned.1.call-start = ((), (), s32[]{:S(2)}) async-start(), calls=%async_computation.16 | async-start | bytes 18874368 | tf_op jit(solution)/shard_map/all_gather | solution.py:153
  20.2 830.1 %all-gather.26.cloned.1.call-start = ((), (), s32[]{:S(2)}) async-start(), calls=%async_computation.17 | async-start | bytes 18874368 | tf_op jit(solution)/shard_map/all_gather | solution.py:154
  24.1 5.8 copy-start.34
  24.1 20.1 copy-start.32
  24.1 1054.7 %all-gather.28.cloned.1.call-start = ((), (), s32[]{:S(2)}) async-start(), calls=%async_computation.18 | async-start | bytes 18874368 | tf_op jit(solution)/shard_map/all_gather | solution.py:155
  30.2 19.6 copy-start.44
  35.4 16.6 copy-start.35
  51.2 269.3 %copy-start.37 = (pred[128,128]{0,1:T(8,128)(4,1)}, pred[128,128]{0,1:T(8,128)(4,1)S(1)}, u32[]{:S(2)}) copy-start(pred[128,128]{0,1:T(8,128)(4,1)S(1)} %fusion.48) | copy-start | bytes 49156
  52.1 190.2 %copy-start.22 = (f32[128,64]{1,0:T(8,128)}, f32[128,64]{1,0:T(8,128)S(1)}, u32[]{:S(2)}) copy-start(f32[128,64]{1,0:T(8,128)S(1)} %get-tuple-element.50) | copy-start | bytes 98308
  66.8 89.4 %copy-start.11 = (f32[2048]{0:T(1024)S(1)}, f32[2048]{0:T(1024)}, u32[]{:S(2)}) copy-start(f32[2048]{0:T(1024)} %param.23) | copy-start | bytes 24580
  66.8 344.0 %all-to-all-start.2 = ((bf16[4,4,72,2048]{3,2,1,0:T(8,128)(2,1)}), bf16[4,4,72,2048]{3,2,1,0:T(8,128)(2,1)}, u32[]{:S(2)}, u32[]{:S(2)}) async-start(bf16[4,4,72,2048]{3,2,1,0:T(8,128)(2,1)} %select_convert_fusion), calls=%async_computation.2 | async-start | bytes 9437184 | tf_op jit(solution)/shard_map/all_to_all | solution.py:173
  74.4 240.6 %copy-start.25 = (f32[128]{0:T(128)}, f32[128]{0:T(128)S(1)}, u32[]{:S(2)}) copy-start(f32[128]{0:T(128)S(1)} %add_rsqrt_fusion.3) | copy-start | bytes 1540
  74.4 87.8 %copy-start.28 = (f32[2048]{0:T(1024)S(1)}, f32[2048]{0:T(1024)}, u32[]{:S(2)}) copy-start(f32[2048]{0:T(1024)} %param.28) | copy-start | bytes 24580
  74.4 161.1 %copy-start.4 = (bf16[4,128,2048]{2,1,0:T(8,128)(2,1)S(1)}, bf16[4,128,2048]{2,1,0:T(8,128)(2,1)}, u32[]{:S(2)}) copy-start(bf16[4,128,2048]{2,1,0:T(8,128)(2,1)} %all-gather.14.cloned.1.call-done) | copy-start | bytes 6291460
  162.5 78.8 %copy-start.30 = (f32[2048]{0:T(1024)S(1)}, f32[2048]{0:T(1024)}, u32[]{:S(2)}) copy-start(f32[2048]{0:T(1024)} %param.27) | copy-start | bytes 24580
  244.6 75.8 %copy-start.13 = (bf16[128,16,64]{2,0,1:T(8,128)(2,1)}, bf16[128,16,64]{2,0,1:T(8,128)(2,1)S(1)}, u32[]{:S(2)}) copy-start(bf16[128,16,64]{2,0,1:T(8,128)(2,1)S(1)} %get-tuple-element.28) | copy-start | bytes 786436
  244.6 75.8 %copy-start.15 = (bf16[128,16,64]{2,0,1:T(8,128)(2,1)}, bf16[128,16,64]{2,0,1:T(8,128)(2,1)S(1)}, u32[]{:S(2)}) copy-start(bf16[128,16,64]{2,0,1:T(8,128)(2,1)S(1)} %get-tuple-element.29) | copy-start | bytes 786436
  248.1 72.3 %copy-start.38 = (f32[16,128]{1,0:T(8,128)}, f32[16,128]{1,0:T(8,128)S(1)}, u32[]{:S(2)}) copy-start(f32[16,128]{1,0:T(8,128)S(1)} %get-tuple-element.55) | copy-start | bytes 24580
  322.9 76.3 %copy-start.10 = (bf16[16,128,128]{2,1,0:T(8,128)(2,1)}, bf16[16,128,128]{2,1,0:T(8,128)(2,1)S(1)}, u32[]{:S(2)}) copy-start(bf16[16,128,128]{2,1,0:T(8,128)(2,1)S(1)} %convolution_convert_fusion.6) | copy-start | bytes 1572868
  410.8 58.3 %all-to-all-start = ((bf16[4,4,72,2048]{3,2,1,0:T(8,128)(2,1)}), bf16[4,4,72,2048]{3,2,1,0:T(8,128)(2,1)}, u32[]{:S(2)}, u32[]{:S(2)}) async-start(bf16[4,4,72,2048]{3,2,1,0:T(8,128)(2,1)} %broadcast_select_fusion), calls=%async_computation | async-start | bytes 9437184 | tf_op jit(solution)/shard_map/all_to_all | solution.py:151
  1127.2 59.4 %all-to-all-start.3 = ((bf16[1,4,288,2048]{3,1,0,2:T(4,128)(2,1)}), bf16[1,4,288,2048]{3,1,0,2:T(4,128)(2,1)}, u32[]{:S(2)}, u32[]{:S(2)}) async-start(bf16[1,4,288,2048]{3,1,0,2:T(4,128)(2,1)} %copy.103), calls=%async_computation.3 | async-start | bytes 9437184 | tf_op jit(solution)/shard_map/all_to_all | solution.py:212
  1150.8 41.5 %copy-start.33 = (f32[1,128,8]{1,2,0:T(8,128)S(1)}, f32[1,128,8]{1,2,0:T(8,128)}, u32[]{:S(2)}) copy-start(f32[1,128,8]{1,2,0:T(8,128)} %param.22) | copy-start | bytes 12292
  1150.8 41.6 %copy-start.36 = (s32[1024,1]{0,1:T(1,128)S(1)}, s32[1024,1]{0,1:T(1,128)}, u32[]{:S(2)}) copy-start(s32[1024,1]{0,1:T(1,128)} %copy-done.35) | copy-start | bytes 12292
  1186.6 58.8 %all-to-all-start.1 = ((bf16[1,4,288,2048]{3,1,0,2:T(4,128)(2,1)}), bf16[1,4,288,2048]{3,1,0,2:T(4,128)(2,1)}, u32[]{:S(2)}, u32[]{:S(2)}) async-start(bf16[1,4,288,2048]{3,1,0,2:T(4,128)(2,1)} %copy.99), calls=%async_computation.1 | async-start | bytes 9437184 | tf_op jit(solution)/shard_map/all_to_all | solution.py:162
  1192.4 242.6 %all-gather.34.cloned.1.call-start = ((), (), s32[]{:S(2)}) async-start(), calls=%async_computation.28 | async-start | bytes 2621440 | tf_op jit(solution)/shard_map/all_gather | solution.py:284
  1273.2 9.3 copy-start.14
  1273.2 9.3 copy-start.16
  1273.2 9.3 copy-start.17
  1273.2 9.3 copy-start.18
  1273.2 9.3 copy-start.39
  1288.8 5.0 slice-start.2
  1291.0 5.7 copy-start.8
  1291.5 5.2 slice-start
  1293.8 5.9 slice-start.4
  1304.1 132.8 %all-gather.32.cloned.1.call-start = ((), (), s32[]{:S(2)}) async-start(), calls=%async_computation.27 | async-start | bytes 2621440 | tf_op jit(solution)/shard_map/all_gather | solution.py:283
  1304.8 332.6 %reduce-scatter.16.cloned.1.call-start = ((), (), s32[]{:S(2)}) async-start(), calls=%async_computation.24 | async-start | bytes 18874368 | tf_op jit(solution)/shard_map/reduce_scatter | solution.py:202
  1319.7 603.8 %reduce-scatter.18.cloned.1.call-start = ((), (), s32[]{:S(2)}) async-start(), calls=%async_computation.25 | async-start | bytes 18874368 | tf_op jit(solution)/shard_map/reduce_scatter | solution.py:205
  1334.7 874.2 %reduce-scatter.20.cloned.1.call-start = ((), (), s32[]{:S(2)}) async-start(), calls=%async_computation.26 | async-start | bytes 18874368 | tf_op jit(solution)/shard_map/reduce_scatter | solution.py:208
  1350.2 1046.1 %reduce-scatter.14.cloned.1.call-start = ((), (), s32[]{:S(2)}) async-start(), calls=%async_computation.23 | async-start | bytes 17301504 | tf_op jit(solution)/shard_map/reduce_scatter | solution.py:276
  1359.4 1224.3 %reduce-scatter.12.cloned.1.call-start = ((), (), s32[]{:S(2)}) async-start(), calls=%async_computation.22 | async-start | bytes 17301504 | tf_op jit(solution)/shard_map/reduce_scatter | solution.py:275
  1368.7 1401.8 %reduce-scatter.10.cloned.1.call-start = ((), (), s32[]{:S(2)}) async-start(), calls=%async_computation.21 | async-start | bytes 17301504 | tf_op jit(solution)/shard_map/reduce_scatter | solution.py:274
  1378.0 1580.6 %reduce-scatter.8.cloned.1.call-start = ((), (), s32[]{:S(2)}) async-start(), calls=%async_computation.20 | async-start | bytes 17301504 | tf_op jit(solution)/shard_map/reduce_scatter | solution.py:273
  (27 other events, 52.7 us)
Sparse Core Ops, SparseCore 0:
  9.6 24.2 all-gather.29
  35.4 22.6 all-gather.13
  61.5 94.6 all-gather.19
  159.5 75.9 all-gather.17
  238.8 76.1 all-gather.15
  318.2 76.1 all-gather.21
  397.2 224.4 all-gather.23
  624.4 225.7 all-gather.25
  853.0 225.7 all-gather.27
  1304.2 21.3 all-gather.33
  1327.8 22.5 all-gather.31
  1354.1 283.3 reduce-scatter.15
  1641.7 281.6 reduce-scatter.17
  1927.1 281.7 reduce-scatter.19
  2211.7 184.6 reduce-scatter.13
  2399.2 184.5 reduce-scatter.11
  2586.6 183.8 reduce-scatter.9
  2773.3 185.2 reduce-scatter.7
where the time goes:
time: 2970 us
  waiting for transfers between devices  2490 us (84%)
  matrix products  205 us (7%)
  local copies, waits for them, and re-layouts  107 us (4%)
  other arithmetic  74.5 us (3%)
  blocking collectives  42.1 us (1%)
    reduce_scatter x1, waiting for transfers between devices, per_device(): lax.psum_scatter(grad_up.astype(jnp.bfloat16), 'dp', scatter_dimension=1,...  282 us
    reduce_scatter x1, waiting for transfers between devices, per_device(): lax.psum_scatter(grad_down.astype(jnp.bfloat16), 'dp', scatter_dimension=...  281 us
    all_gather x1, waiting for transfers between devices, per_device(): lax.all_gather(w_down.astype(jnp.bfloat16), 'dp', axis=1, tiled=True)  215 us
    all_gather x1, waiting for transfers between devices, per_device(): lax.all_gather(w_up.astype(jnp.bfloat16), 'dp', axis=1, tiled=True)  215 us
    reduce_scatter x1, waiting for transfers between devices, per_device(): lax.psum_scatter(grad_gate.astype(jnp.bfloat16), 'dp', scatter_dimension=...  199 us
    reduce_scatter x1, waiting for transfers between devices, per_device(): lax.psum_scatter(grad_query_mat, ('dp', 'expert'), scatter_dimension=0, t...  188 us
    reduce_scatter x1, waiting for transfers between devices, per_device(): lax.psum_scatter(grad_value_mat, ('dp', 'expert'), scatter_dimension=0, t...  187 us
    reduce_scatter x1, waiting for transfers between devices, per_device(): lax.psum_scatter(grad_key_mat, ('dp', 'expert'), scatter_dimension=0, til...  187 us
  transfers between devices with their start and end apart: 22, of which 17 were waited for; matrix products, arithmetic and copies ran while one was open for 9% of the time, Pallas kernels for 0%

commit v1 on v0

--- a/solution.py
+++ b/solution.py
@@ -6,6 +6,30 @@
 
 HEADS = 16
 epsilon = 1e-05
+
+
+def edit_series_all(w_in, along_dim):
+    chip_axis = "dp"
+    piece_out = lax.psum(1, chip_axis)
+    response = lax.axis_index(chip_axis)
+    y, local_out, v_now = (piece_out, response, w_in.shape[along_dim])
+    lanes = [i * y if ii == along_dim else i for ii, i in enumerate(w_in.shape)]
+    local_part = jnp.zeros(lanes, w_in.dtype)
+    item_now = lax.dynamic_update_slice_in_dim(local_part, w_in, local_out * v_now, axis=along_dim)
+    e_now = oldest = w_in
+    for tick in range(1, y // 2 + 1):
+        e_next = list(map(lambda ii: (ii, (ii + 1) % y), range(y)))
+        e_now = lax.ppermute(e_now, chip_axis, e_next)
+        item_now = lax.dynamic_update_slice_in_dim(
+            item_now, e_now, (local_out - tick) % y * v_now, axis=along_dim
+        )
+        if 2 * tick < y:
+            big = map(lambda ii: (ii, (ii - 1) % y), range(y))
+            oldest = lax.ppermute(oldest, chip_axis, list(big))
+            item_now = lax.dynamic_update_slice_in_dim(
+                item_now, oldest, (local_out + tick) % y * v_now, axis=along_dim
+            )
+    return item_now
 
 
 def norm_scale(values):
@@ -151,7 +175,7 @@
     received = lax.all_to_all(sending, "expert", split_axis=0, concat_axis=2, tiled=True)[0]
     expert_mats = (
         lax.all_gather(w_gate.astype(jnp.bfloat16), "dp", axis=1, tiled=True),
-        lax.all_gather(w_up.astype(jnp.bfloat16), "dp", axis=1, tiled=True),
+        edit_series_all(w_up.astype(jnp.bfloat16), 1),
         lax.all_gather(w_down.astype(jnp.bfloat16), "dp", axis=1, tiled=True),
     )
     gate_mat, up_mat, down_mat = expert_mats

time: 2970 us -> 3080 us (1.037)
  waiting for transfers between devices: 2490 us -> 2560 us
    ppermute x0 -> x7, waiting for transfers between devices: none -> 242 us  [the longest x4 155 us: edit_series_all(): e_now = lax.ppermute(e_now, chip_axis, e_next)]
    all_gather x1, waiting for transfers between devices: 73 us -> 0.01 us  [per_device(): lax.all_gather(w_query.astype(jnp.bfloat16), ('dp', 'expert'), axis=0, ti...]
    all_to_all x1, waiting for transfers between devices: 47.6 us -> 0.01 us  [per_device(): lax.all_to_all(sending, 'expert', split_axis=0, concat_axis=2, tiled=True)]
  transfers between devices with their start and end apart: 22 -> 29, of which waited for: 17 -> 18; matrix products, arithmetic and copies ran while one was open for 9% -> 11% of each run, Pallas kernels for 0% -> 0%
where the time goes in v1:
time: 3080 us; the launch traced here: 3070 us
  waiting for transfers between devices  2560 us (83%)
  matrix products  206 us (7%)
  local copies, waits for them, and re-layouts  136 us (4%)
  other arithmetic  73 us (2%)
  blocking collectives  42.2 us (1%)
  starting transfers between devices  34.5 us (1%)
    reduce_scatter x1, waiting for transfers between devices, per_device(): lax.psum_scatter(grad_up.astype(jnp.bfloat16), 'dp', scatter_dimension=1,...  282 us
    reduce_scatter x1, waiting for transfers between devices, per_device(): lax.psum_scatter(grad_down.astype(jnp.bfloat16), 'dp', scatter_dimension=...  281 us
    all_gather x1, waiting for transfers between devices, per_device(): lax.all_gather(w_down.astype(jnp.bfloat16), 'dp', axis=1, tiled=True)  215 us
    reduce_scatter x1, waiting for transfers between devices, per_device(): lax.psum_scatter(grad_gate.astype(jnp.bfloat16), 'dp', scatter_dimension=...  199 us
    reduce_scatter x1, waiting for transfers between devices, per_device(): lax.psum_scatter(grad_value_mat, ('dp', 'expert'), scatter_dimension=0, t...  188 us
    reduce_scatter x1, waiting for transfers between devices, per_device(): lax.psum_scatter(grad_query_mat, ('dp', 'expert'), scatter_dimension=0, t...  187 us
    all_gather x1, waiting for transfers between devices, per_device(): lax.all_gather(w_up.astype(jnp.bfloat16), 'dp', axis=1, tiled=True)  187 us
    reduce_scatter x1, waiting for transfers between devices, per_device(): lax.psum_scatter(grad_key_mat, ('dp', 'expert'), scatter_dimension=0, til...  186 us
  transfers between devices with their start and end apart: 29, of which 18 were waited for; matrix products, arithmetic and copies ran while one was open for 11% of the time, Pallas kernels for 0%

profile of v1, /device:TPU:3, one launch (start us, length us, event | category | flops | bytes accessed | tf_op | source)
XLA Modules:
  0.0 3074.1 jit_solution(8459145906041783301)
XLA Ops:
  24.1 6.7 broadcast_in_dim.62
  49.2 87.8 %collective-permute-done = bf16[4,256,1024]{2,1,0:T(8,128)(2,1)} collective-permute-done((bf16[4,256,1024]{2,1,0:T(8,128)(2,1)}, bf16[4,256,1024]{2,1,0:T(8,128)(2,1)}, u32[]{:S(2)}, u32[]{:S(2)}) %collective-permute-start) | collective-permute-done | bytes 2097184 | tf_op jit(solution)/shard_map/ppermute | solution.py:22
  149.4 6.8 gather_fusion.3
  156.2 6.7 select_convert_fusion
  162.9 9.9 all-to-all-start.2
  174.0 67.0 %collective-permute-done.2 = bf16[4,256,1024]{2,1,0:T(8,128)(2,1)} collective-permute-done((bf16[4,256,1024]{2,1,0:T(8,128)(2,1)}, bf16[4,256,1024]{2,1,0:T(8,128)(2,1)}, u32[]{:S(2)}, u32[]{:S(2)}) %collective-permute-start.2) | collective-permute-done | bytes 2097184 | tf_op jit(solution)/shard_map/ppermute | solution.py:22
  248.0 79.3 %all-gather.20.cloned.1.call-done = bf16[2048,2048]{1,0:T(8,128)(2,1)} async-done(((bf16[64,2048]{1,0:T(8,128)(2,1)}), bf16[2048,2048]{1,0:T(8,128)(2,1)}) %all-gather.20.cloned.1.call-update) | async-done | bytes 8388624 | tf_op jit(solution)/shard_map/all_gather | solution.py:125
  340.0 67.0 %all-gather.16.cloned.1.call-done = bf16[2048,2048]{1,0:T(8,128)(2,1)} async-done(((bf16[64,2048]{1,0:T(8,128)(2,1)}), bf16[2048,2048]{1,0:T(8,128)(2,1)}) %all-gather.16.cloned.1.call-update) | async-done | bytes 8388624 | tf_op jit(solution)/shard_map/all_gather | solution.py:126
  415.1 71.5 %all-gather.22.cloned.1.call-done = bf16[2048,2048]{1,0:T(8,128)(2,1)} async-done(((bf16[64,2048]{1,0:T(8,128)(2,1)}), bf16[2048,2048]{1,0:T(8,128)(2,1)}) %all-gather.22.cloned.1.call-update) | async-done | bytes 8388624 | tf_op jit(solution)/shard_map/all_gather | solution.py:127
  491.5 5.9 gather_fusion
  526.0 87.1 %collective-permute-done.5 = bf16[4,256,1024]{2,1,0:T(8,128)(2,1)} collective-permute-done((bf16[4,256,1024]{2,1,0:T(8,128)(2,1)}, bf16[4,256,1024]{2,1,0:T(8,128)(2,1)}, u32[]{:S(2)}, u32[]{:S(2)}) %collective-permute-start.5) | collective-permute-done | bytes 2097184 | tf_op jit(solution)/shard_map/ppermute | solution.py:28
  616.2 5.9 copy.102
  630.5 127.9 %all-gather.24.cloned.1.call-done = bf16[4,2048,1024]{2,1,0:T(8,128)(2,1)} async-done(((bf16[4,256,1024]{2,1,0:T(8,128)(2,1)}), bf16[4,2048,1024]{2,1,0:T(8,128)(2,1)}) %all-gather.24.cloned.1.call-update) | async-done | bytes 16777232 | tf_op jit(solution)/shard_map/all_gather | solution.py:177
  758.4 13.1 fusion.79
  771.5 215.5 %all-gather.26.cloned.1.call-done = bf16[4,1024,2048]{2,1,0:T(8,128)(2,1)} async-done(((bf16[4,128,2048]{2,1,0:T(8,128)(2,1)}), bf16[4,1024,2048]{2,1,0:T(8,128)(2,1)}) %all-gather.26.cloned.1.call-update) | async-done | bytes 16777232 | tf_op jit(solution)/shard_map/all_gather | solution.py:179
  987.0 11.7 fusion.80
  998.6 17.8 multiply_convert_fusion
  1016.4 11.5 fusion.81
  1028.0 187.0 %all-gather.30.cloned.1.call-done = bf16[4,2048,1024]{2,1,0:T(8,128)(2,1)} async-done(((bf16[4,256,1024]{2,1,0:T(8,128)(2,1)}), bf16[4,2048,1024]{2,1,0:T(8,128)(2,1)}) %all-gather.30.cloned.1.call-update) | async-done | bytes 16777232 | tf_op jit(solution)/shard_map/all_gather | solution.py:200
  1215.0 13.7 fusion.2
  1228.7 8.1 copy.103
  1236.8 6.4 all-to-all-start.3
  1243.2 11.5 convert_bitcast_fusion
  1254.7 5.8 copy.99
  1260.4 35.8 %all-to-all-done.3 = bf16[1,4,288,2048]{3,1,0,2:T(4,128)(2,1)} async-done(((bf16[1,4,288,2048]{3,1,0,2:T(4,128)(2,1)}), bf16[1,4,288,2048]{3,1,0,2:T(4,128)(2,1)}, u32[]{:S(2)}, u32[]{:S(2)}) %all-to-all-start.3) | async-done | bytes 4718624 | tf_op jit(solution)/shard_map/all_to_all | solution.py:236
  1296.2 5.9 all-to-all-start.1
  1302.2 7.1 copy.104
  1309.3 11.9 gather_fusion.4
  1326.6 28.4 all-to-all-done.1
  1355.1 7.0 copy.100
  1362.1 11.9 gather_fusion.1
  1374.1 6.5 fusion.1
  1382.9 7.2 convolution_convert_fusion.3
  1414.5 14.7 convolution_convert_fusion.2
  1429.3 14.9 convolution_convert_fusion.1
  1444.3 15.4 convolution_convert_fusion
  1459.8 9.1 fusion.37
  1470.0 8.2 fusion.28
  1479.2 8.3 fusion.67
  1488.5 8.3 fusion.69
  1500.0 42.2 %all-reduce.4 = (f32[2048]{0:T(1024)S(1)}, f32[2048]{0:T(1024)S(1)}, f32[2048]{0:T(1024)S(1)}, f32[2048]{0:T(1024)S(1)}) all-reduce(f32[2048]{0:T(1024)S(1)} %get-tuple-element.13, f32[2048]{0:T(1024)S(1)} %get-tuple-element.19, f32[2048]{0:T(1024)S(1)} %get-tuple-element.17, ...), channel_id=4, replica_groups=mesh['dp'=8,'expert'=4] {'dp','expert'}, use_global_device_ids=true, to_apply=%region_20.21.clone | all-reduce | flops 8192 | bytes 65536
  1548.4 198.7 %reduce-scatter.16.cloned.1.call-done = bf16[4,256,1024]{2,1,0:T(8,128)(2,1)} async-done(((bf16[4,2048,1024]{2,1,0:T(8,128)(2,1)}), bf16[4,256,1024]{2,1,0:T(8,128)(2,1)}) %reduce-scatter.16.cloned.1.call-update) | async-done | bytes 2097168 | tf_op jit(solution)/shard_map/reduce_scatter | solution.py:226
  1751.2 281.9 %reduce-scatter.18.cloned.1.call-done = bf16[4,256,1024]{2,1,0:T(8,128)(2,1)} async-done(((bf16[4,2048,1024]{2,1,0:T(8,128)(2,1)}), bf16[4,256,1024]{2,1,0:T(8,128)(2,1)}) %reduce-scatter.18.cloned.1.call-update) | async-done | bytes 2097168 | tf_op jit(solution)/shard_map/reduce_scatter | solution.py:229
  2037.2 281.2 %reduce-scatter.20.cloned.1.call-done = bf16[4,128,2048]{2,1,0:T(8,128)(2,1)} async-done(((bf16[4,1024,2048]{2,1,0:T(8,128)(2,1)}), bf16[4,128,2048]{2,1,0:T(8,128)(2,1)}) %reduce-scatter.20.cloned.1.call-update) | async-done | bytes 2097168 | tf_op jit(solution)/shard_map/reduce_scatter | solution.py:232
  2322.6 182.7 %reduce-scatter.14.cloned.1.call-done = f32[64,2048]{1,0:T(8,128)} async-done(((f32[2048,2048]{1,0:T(8,128)}), f32[64,2048]{1,0:T(8,128)}) %reduce-scatter.14.cloned.1.call-update) | async-done | bytes 524304 | tf_op jit(solution)/shard_map/reduce_scatter | solution.py:300
  2505.3 187.8 %reduce-scatter.12.cloned.1.call-done = f32[64,2048]{1,0:T(8,128)} async-done(((f32[2048,2048]{1,0:T(8,128)}), f32[64,2048]{1,0:T(8,128)}) %reduce-scatter.12.cloned.1.call-update) | async-done | bytes 524304 | tf_op jit(solution)/shard_map/reduce_scatter | solution.py:299
  2693.1 186.5 %reduce-scatter.10.cloned.1.call-done = f32[64,2048]{1,0:T(8,128)} async-done(((f32[2048,2048]{1,0:T(8,128)}), f32[64,2048]{1,0:T(8,128)}) %reduce-scatter.10.cloned.1.call-update) | async-done | bytes 524304 | tf_op jit(solution)/shard_map/reduce_scatter | solution.py:298
  2879.6 187.4 %reduce-scatter.8.cloned.1.call-done = f32[64,2048]{1,0:T(8,128)} async-done(((f32[2048,2048]{1,0:T(8,128)}), f32[64,2048]{1,0:T(8,128)}) %reduce-scatter.8.cloned.1.call-update) | async-done | bytes 524304 | tf_op jit(solution)/shard_map/reduce_scatter | solution.py:297
  (272 shorter events, 174.1 us)
Async XLA Ops:
  7.2 141.1 %all-gather.28.cloned.1.call-start = ((), (), s32[]{:S(2)}) async-start(), calls=%async_computation.18 | async-start | bytes 2621440 | tf_op jit(solution)/shard_map/all_gather | solution.py:112
  7.9 164.8 %all-gather.14.cloned.1.call-start = ((), (), s32[]{:S(2)}) async-start(), calls=%async_computation.11 | async-start | bytes 2621440 | tf_op jit(solution)/shard_map/all_gather | solution.py:111
  8.7 233.0 %all-gather.18.cloned.1.call-start = ((), (), s32[]{:S(2)}) async-start(), calls=%async_computation.13 | async-start | bytes 8650752 | tf_op jit(solution)/shard_map/all_gather | solution.py:124
  10.5 316.8 %all-gather.20.cloned.1.call-start = ((), (), s32[]{:S(2)}) async-start(), calls=%async_computation.14 | async-start | bytes 8650752 | tf_op jit(solution)/shard_map/all_gather | solution.py:125
  12.4 394.7 %all-gather.16.cloned.1.call-start = ((), (), s32[]{:S(2)}) async-start(), calls=%async_computation.12 | async-start | bytes 8650752 | tf_op jit(solution)/shard_map/all_gather | solution.py:126
  14.2 472.3 %all-gather.22.cloned.1.call-start = ((), (), s32[]{:S(2)}) async-start(), calls=%async_computation.15 | async-start | bytes 8650752 | tf_op jit(solution)/shard_map/all_gather | solution.py:127
  16.1 742.4 %all-gather.24.cloned.1.call-start = ((), (), s32[]{:S(2)}) async-start(), calls=%async_computation.16 | async-start | bytes 18874368 | tf_op jit(solution)/shard_map/all_gather | solution.py:177
  20.2 966.8 %all-gather.26.cloned.1.call-start = ((), (), s32[]{:S(2)}) async-start(), calls=%async_computation.17 | async-start | bytes 18874368 | tf_op jit(solution)/shard_map/all_gather | solution.py:179
  24.1 1190.9 %all-gather.30.cloned.1.call-start = ((), (), s32[]{:S(2)}) async-start(), calls=%async_computation.19 | async-start | bytes 18874368 | tf_op jit(solution)/shard_map/all_gather | solution.py:200
  30.8 106.4 %copy-start.47 = (s32[1,4]{1,0:T(1,128)S(1)}, s32[1,4]{1,0:T(1,128)}, u32[]{:S(2)}) copy-start(s32[1,4]{1,0:T(1,128)} %param.20) | copy-start | bytes 52
  30.8 108.3 %copy-start.34 = (f32[1,128,8]{1,2,0:T(8,128)S(1)}, f32[1,128,8]{1,2,0:T(8,128)}, u32[]{:S(2)}) copy-start(f32[1,128,8]{1,2,0:T(8,128)} %param.22) | copy-start | bytes 12292
  33.5 103.5 %collective-permute-start = (bf16[4,256,1024]{2,1,0:T(8,128)(2,1)}, bf16[4,256,1024]{2,1,0:T(8,128)(2,1)}, u32[]{:S(2)}, u32[]{:S(2)}) collective-permute-start(bf16[4,256,1024]{2,1,0:T(8,128)(2,1)} %get-tuple-element.26), channel_id=1, source_target_pairs={{0,4},{4,8},{8,12},{12,16},{16,20},{20,24},{24,28},{28,0},{1,5},{5... | collective-permute-start | bytes 6291464 | tf_op jit(solution)/shard_map/ppermute | solution.py:22
  34.8 112.2 %collective-permute-start.1 = (bf16[4,256,1024]{2,1,0:T(8,128)(2,1)}, bf16[4,256,1024]{2,1,0:T(8,128)(2,1)}, u32[]{:S(2)}, u32[]{:S(2)}) collective-permute-start(bf16[4,256,1024]{2,1,0:T(8,128)(2,1)} %get-tuple-element.26), channel_id=1, source_target_pairs={{0,28},{4,0},{8,4},{12,8},{16,12},{20,16},{24,20},{28,24},{1,29},{... | collective-permute-start | bytes 6291464 | tf_op jit(solution)/shard_map/ppermute | solution.py:28
  35.3 109.4 %copy-start.46 = (s32[4]{0:T(128)S(1)}, s32[4]{0:T(128)}, u32[]{:S(2)}) copy-start(s32[4]{0:T(128)} %param.19) | copy-start | bytes 52
  40.5 107.8 %copy-start.37 = (s32[1024,1]{0,1:T(1,128)}, s32[1024,1]{0,1:T(1,128)S(1)}, u32[]{:S(2)}) copy-start(s32[1024,1]{0,1:T(1,128)S(1)} %compare_select_fusion) | copy-start | bytes 12292
  137.0 103.9 %collective-permute-start.2 = (bf16[4,256,1024]{2,1,0:T(8,128)(2,1)}, bf16[4,256,1024]{2,1,0:T(8,128)(2,1)}, u32[]{:S(2)}, u32[]{:S(2)}) collective-permute-start(bf16[4,256,1024]{2,1,0:T(8,128)(2,1)} %collective-permute-done), channel_id=1, source_target_pairs={{0,4},{4,8},{8,12},{12,16},{16,20},{20,24},{24,28},{28,0},{1,5},{5... | collective-permute-start | bytes 6291464 | tf_op jit(solution)/shard_map/ppermute | solution.py:22
  146.0 266.6 %copy-start.39 = (pred[128,128]{0,1:T(8,128)(4,1)}, pred[128,128]{0,1:T(8,128)(4,1)S(1)}, u32[]{:S(2)}) copy-start(pred[128,128]{0,1:T(8,128)(4,1)S(1)} %fusion.48) | copy-start | bytes 49156
  146.9 187.2 %copy-start.24 = (f32[128,64]{1,0:T(8,128)}, f32[128,64]{1,0:T(8,128)S(1)}, u32[]{:S(2)}) copy-start(f32[128,64]{1,0:T(8,128)S(1)} %get-tuple-element.52) | copy-start | bytes 98308
  146.9 361.1 %collective-permute-start.3 = (bf16[4,256,1024]{2,1,0:T(8,128)(2,1)}, bf16[4,256,1024]{2,1,0:T(8,128)(2,1)}, u32[]{:S(2)}, u32[]{:S(2)}) collective-permute-start(bf16[4,256,1024]{2,1,0:T(8,128)(2,1)} %collective-permute-done.1), channel_id=1, source_target_pairs={{0,28},{4,0},{8,4},{12,8},{16,12},{20,16},{24,20},{28,24},{1,29},{... | collective-permute-start | bytes 6291464 | tf_op jit(solution)/shard_map/ppermute | solution.py:28
  162.9 78.8 %copy-start.13 = (f32[2048]{0:T(1024)S(1)}, f32[2048]{0:T(1024)}, u32[]{:S(2)}) copy-start(f32[2048]{0:T(1024)} %param.23) | copy-start | bytes 24580
  162.9 340.0 %all-to-all-start.2 = ((bf16[4,4,72,2048]{3,2,1,0:T(8,128)(2,1)}), bf16[4,4,72,2048]{3,2,1,0:T(8,128)(2,1)}, u32[]{:S(2)}, u32[]{:S(2)}) async-start(bf16[4,4,72,2048]{3,2,1,0:T(8,128)(2,1)} %select_convert_fusion), calls=%async_computation.2 | async-start | bytes 9437184 | tf_op jit(solution)/shard_map/all_to_all | solution.py:197
  174.0 233.1 %copy-start.27 = (f32[128]{0:T(128)}, f32[128]{0:T(128)S(1)}, u32[]{:S(2)}) copy-start(f32[128]{0:T(128)S(1)} %add_rsqrt_fusion.3) | copy-start | bytes 1540
  174.0 73.7 %copy-start.32 = (f32[2048]{0:T(1024)S(1)}, f32[2048]{0:T(1024)}, u32[]{:S(2)}) copy-start(f32[2048]{0:T(1024)} %param.27) | copy-start | bytes 24580
  174.0 153.3 %copy-start.4 = (bf16[4,128,2048]{2,1,0:T(8,128)(2,1)S(1)}, bf16[4,128,2048]{2,1,0:T(8,128)(2,1)}, u32[]{:S(2)}) copy-start(bf16[4,128,2048]{2,1,0:T(8,128)(2,1)} %all-gather.14.cloned.1.call-done) | copy-start | bytes 6291460
  241.0 267.5 %collective-permute-start.4 = (bf16[4,256,1024]{2,1,0:T(8,128)(2,1)}, bf16[4,256,1024]{2,1,0:T(8,128)(2,1)}, u32[]{:S(2)}, u32[]{:S(2)}) collective-permute-start(bf16[4,256,1024]{2,1,0:T(8,128)(2,1)} %collective-permute-done.2), channel_id=1, source_target_pairs={{0,4},{4,8},{8,12},{12,16},{16,20},{20,24},{24,28},{28,0},{1,5},{5... | collective-permute-start | bytes 6291464 | tf_op jit(solution)/shard_map/ppermute | solution.py:22
  248.0 85.1 %copy-start.30 = (f32[2048]{0:T(1024)S(1)}, f32[2048]{0:T(1024)}, u32[]{:S(2)}) copy-start(f32[2048]{0:T(1024)} %param.28) | copy-start | bytes 24580
  336.5 76.1 %copy-start.15 = (bf16[128,16,64]{2,0,1:T(8,128)(2,1)}, bf16[128,16,64]{2,0,1:T(8,128)(2,1)S(1)}, u32[]{:S(2)}) copy-start(bf16[128,16,64]{2,0,1:T(8,128)(2,1)S(1)} %get-tuple-element.30) | copy-start | bytes 786436
  336.5 76.1 %copy-start.17 = (bf16[128,16,64]{2,0,1:T(8,128)(2,1)}, bf16[128,16,64]{2,0,1:T(8,128)(2,1)S(1)}, u32[]{:S(2)}) copy-start(bf16[128,16,64]{2,0,1:T(8,128)(2,1)S(1)} %get-tuple-element.31) | copy-start | bytes 786436
  340.0 72.6 %copy-start.40 = (f32[16,128]{1,0:T(8,128)}, f32[16,128]{1,0:T(8,128)S(1)}, u32[]{:S(2)}) copy-start(f32[16,128]{1,0:T(8,128)S(1)} %get-tuple-element.57) | copy-start | bytes 24580
  415.1 76.3 %copy-start.12 = (bf16[16,128,128]{2,1,0:T(8,128)(2,1)}, bf16[16,128,128]{2,1,0:T(8,128)(2,1)S(1)}, u32[]{:S(2)}) copy-start(bf16[16,128,128]{2,1,0:T(8,128)(2,1)S(1)} %convolution_convert_fusion.6) | copy-start | bytes 1572868
  502.9 122.5 %all-to-all-start = ((bf16[4,4,72,2048]{3,2,1,0:T(8,128)(2,1)}), bf16[4,4,72,2048]{3,2,1,0:T(8,128)(2,1)}, u32[]{:S(2)}, u32[]{:S(2)}) async-start(bf16[4,4,72,2048]{3,2,1,0:T(8,128)(2,1)} %broadcast_select_fusion), calls=%async_computation | async-start | bytes 9437184 | tf_op jit(solution)/shard_map/all_to_all | solution.py:175
  508.1 105.0 %collective-permute-start.5 = (bf16[4,256,1024]{2,1,0:T(8,128)(2,1)}, bf16[4,256,1024]{2,1,0:T(8,128)(2,1)}, u32[]{:S(2)}, u32[]{:S(2)}) collective-permute-start(bf16[4,256,1024]{2,1,0:T(8,128)(2,1)} %collective-permute-done.3), channel_id=1, source_target_pairs={{0,28},{4,0},{8,4},{12,8},{16,12},{20,16},{24,20},{28,24},{1,29},{... | collective-permute-start | bytes 6291464 | tf_op jit(solution)/shard_map/ppermute | solution.py:28
  508.5 113.6 %collective-permute-start.6 = (bf16[4,256,1024]{2,1,0:T(8,128)(2,1)}, bf16[4,256,1024]{2,1,0:T(8,128)(2,1)}, u32[]{:S(2)}, u32[]{:S(2)}) collective-permute-start(bf16[4,256,1024]{2,1,0:T(8,128)(2,1)} %collective-permute-done.4), channel_id=1, source_target_pairs={{0,4},{4,8},{8,12},{12,16},{16,20},{20,24},{24,28},{28,0},{1,5},{5... | collective-permute-start | bytes 6291464 | tf_op jit(solution)/shard_map/ppermute | solution.py:22
  987.0 11.7 copy-start.8
  1236.8 59.4 %all-to-all-start.3 = ((bf16[1,4,288,2048]{3,1,0,2:T(4,128)(2,1)}), bf16[1,4,288,2048]{3,1,0,2:T(4,128)(2,1)}, u32[]{:S(2)}, u32[]{:S(2)}) async-start(bf16[1,4,288,2048]{3,1,0,2:T(4,128)(2,1)} %copy.103), calls=%async_computation.3 | async-start | bytes 9437184 | tf_op jit(solution)/shard_map/all_to_all | solution.py:236
  1260.4 41.6 %copy-start.35 = (f32[1,128,8]{1,2,0:T(8,128)S(1)}, f32[1,128,8]{1,2,0:T(8,128)}, u32[]{:S(2)}) copy-start(f32[1,128,8]{1,2,0:T(8,128)} %param.22) | copy-start | bytes 12292
  1260.4 41.7 %copy-start.38 = (s32[1024,1]{0,1:T(1,128)S(1)}, s32[1024,1]{0,1:T(1,128)}, u32[]{:S(2)}) copy-start(s32[1024,1]{0,1:T(1,128)} %copy-done.37) | copy-start | bytes 12292
  1296.2 58.9 %all-to-all-start.1 = ((bf16[1,4,288,2048]{3,1,0,2:T(4,128)(2,1)}), bf16[1,4,288,2048]{3,1,0,2:T(4,128)(2,1)}, u32[]{:S(2)}, u32[]{:S(2)}) async-start(bf16[1,4,288,2048]{3,1,0,2:T(4,128)(2,1)} %copy.99), calls=%async_computation.1 | async-start | bytes 9437184 | tf_op jit(solution)/shard_map/all_to_all | solution.py:186
  1302.0 242.6 %all-gather.34.cloned.1.call-start = ((), (), s32[]{:S(2)}) async-start(), calls=%async_computation.28 | async-start | bytes 2621440 | tf_op jit(solution)/shard_map/all_gather | solution.py:308
  1382.9 9.3 copy-start.41
  1413.7 132.8 %all-gather.32.cloned.1.call-start = ((), (), s32[]{:S(2)}) async-start(), calls=%async_computation.27 | async-start | bytes 2621440 | tf_op jit(solution)/shard_map/all_gather | solution.py:307
  1414.4 332.7 %reduce-scatter.16.cloned.1.call-start = ((), (), s32[]{:S(2)}) async-start(), calls=%async_computation.24 | async-start | bytes 18874368 | tf_op jit(solution)/shard_map/reduce_scatter | solution.py:226
  1429.2 603.9 %reduce-scatter.18.cloned.1.call-start = ((), (), s32[]{:S(2)}) async-start(), calls=%async_computation.25 | async-start | bytes 18874368 | tf_op jit(solution)/shard_map/reduce_scatter | solution.py:229
  1444.3 874.2 %reduce-scatter.20.cloned.1.call-start = ((), (), s32[]{:S(2)}) async-start(), calls=%async_computation.26 | async-start | bytes 18874368 | tf_op jit(solution)/shard_map/reduce_scatter | solution.py:232
  1459.7 1045.6 %reduce-scatter.14.cloned.1.call-start = ((), (), s32[]{:S(2)}) async-start(), calls=%async_computation.23 | async-start | bytes 17301504 | tf_op jit(solution)/shard_map/reduce_scatter | solution.py:300
  1468.9 1224.2 %reduce-scatter.12.cloned.1.call-start = ((), (), s32[]{:S(2)}) async-start(), calls=%async_computation.22 | async-start | bytes 17301504 | tf_op jit(solution)/shard_map/reduce_scatter | solution.py:299
  1478.2 1401.4 %reduce-scatter.10.cloned.1.call-start = ((), (), s32[]{:S(2)}) async-start(), calls=%async_computation.21 | async-start | bytes 17301504 | tf_op jit(solution)/shard_map/reduce_scatter | solution.py:298
  1487.5 1579.6 %reduce-scatter.8.cloned.1.call-start = ((), (), s32[]{:S(2)}) async-start(), calls=%async_computation.20 | async-start | bytes 17301504 | tf_op jit(solution)/shard_map/reduce_scatter | solution.py:297
  (36 other events, 118.5 us)
Sparse Core Ops, SparseCore 0:
  9.6 24.2 all-gather.27
  35.4 22.5 all-gather.13
  61.5 156.5 all-gather.17
  221.4 105.9 all-gather.19
  330.6 76.4 all-gather.15
  410.4 76.1 all-gather.21
  489.3 269.0 all-gather.23
  761.2 225.7 all-gather.25
  989.2 225.7 all-gather.29
  1413.8 21.3 all-gather.33
  1437.4 22.5 all-gather.31
  1463.6 283.4 reduce-scatter.15
  1751.4 281.6 reduce-scatter.17
  2036.8 281.6 reduce-scatter.19
  2321.2 183.9 reduce-scatter.13
  2508.1 184.9 reduce-scatter.11
  2695.9 183.6 reduce-scatter.9
  2882.4 184.5 reduce-scatter.7
